TPU v7x, 256 devices: a whole 4x4x8 slice. The times are simulated.
256 devices in a mesh: blk: 64 (over x, z_lo, y), rep: 4 (over z_hi, core).
Axes of the slice: x: 4, y: 4, z: 8 (z_hi: 2, z_lo: 4; z = z_hi * 4 + z_lo), core: 2. Of those that a mesh axis runs over, the one named last changes fastest.
Arguments:
- node_feats: float32 [32768, 256], P('blk'), may hold values from -6 to 6
- operator_tiles: float32 [256, 16, 128, 128], P('blk', 'rep'), may hold values from -0.125 to 0.125
- tile_cols: int32 [256, 16], P('blk', 'rep'), may hold values from 0 to 255, as said below
- weight: float32 [256, 256], replicated, may hold values from -0.375 to 0.375
- layer_bias: float32 [256], replicated, may hold values from -3 to 3
- cotangent: float32 [32768, 256], P(('blk', 'rep')), may hold values from -6 to 6
Outputs:
- layer_out: float32 [32768, 256], P(('blk', 'rep'))
- grad_feats: float32 [32768, 256], P(('blk', 'rep'))
- grad_weight: float32 [256, 256], replicated
- grad_bias: float32 [256], replicated
Inputs may be any that keep to these rules, and one draw needn't show every extreme that they name: `tile_cols`: owner of block j is j // 4, among 64 owners on a closed cycle. Slots r * 4 to (r + 1) * 4 - 1 of row block i name blocks whose owner lies at cycle distance (owner of i minus owner of the column, modulo the number of owners) from r * 16 to (r + 1) * 16 - 1. Slot 0 of row block i names block i itself. Entries may repeat within a row block.
All inputs are finite; a program needn't handle non-finite values.
Results may differ from a plain program's by a relative error of at most 0.0003.
Values sent between devices are 32-bit elements; how exact they have to be, the bound alone decides.
No kernel may reach another device: no remote copies, remote signals or barrier semaphores. Data moves between devices by JAX's collectives and lax.ppermute only.
A program may use at most 64 MiB of HBM per device.

v0:
```python
import math
import jax
import jax.numpy as jnp
from jax import lax
from jax.sharding import PartitionSpec as P

TOP_PRECISION = lax.Precision.HIGHEST


def shifted_2(value, axis, steps):
    count = lax.axis_size(axis)
    pairs = [(source, (source + steps) % count) for source in range(count)]
    return lax.ppermute(value, axis, pairs)


def body(node_feats, operator_tiles, tile_cols, weight, layer_bias, cotangent):
    cycle_size = lax.axis_size("blk")
    rep_size = lax.axis_size("rep")
    window = cycle_size // rep_size
    position = lax.axis_index("blk")
    replica = lax.axis_index("rep")
    offset = replica * window
    blocks, slot_count, tile_size, _ = operator_tiles.shape
    width = node_feats.shape[1]
    row_count = blocks * tile_size
    owners = tile_cols // blocks
    within = tile_cols % blocks
    distance = jnp.mod(position - owners, cycle_size) - offset
    columns = jnp.arange(blocks, dtype=jnp.int32)
    sections = jnp.arange(window, dtype=jnp.int32)
    chosen = (
        (distance[:, :, None, None] == sections[None, None, :, None])
        & (within[:, :, None, None] == columns[None, None, None, :])
    ).astype(jnp.float32)

    def reshape_to_blocks(rows):
        return rows.reshape(blocks, tile_size, width)

    def store(stacked, section_no, current):
        return lax.dynamic_update_index_in_dim(stacked, reshape_to_blocks(current), section_no, 0)

    aligned = node_feats
    for bit_pos in range(rep_size.bit_length() - 1):
        shifted = shifted_2(aligned, "blk", window << bit_pos)
        aligned = jnp.where((replica >> bit_pos) % 2 == 1, shifted, aligned)
    empty = jnp.zeros((window, blocks, tile_size, width), jnp.float32)

    def advance(section_no, loop_state):
        current, stacked = loop_state
        current = shifted_2(current, "blk", 1)
        return (current, store(stacked, section_no, current))

    _, received = lax.fori_loop(1, window, advance, (aligned, store(empty, 0, aligned)))
    selected_tiles = jnp.einsum("iksc,scbd->ikbd", chosen, received, precision=TOP_PRECISION)
    partial_aggregate = jnp.einsum(
        "uzrj,uzje->ure", operator_tiles, selected_tiles, precision=TOP_PRECISION
    ).reshape(row_count, width)
    aggregated = lax.psum_scatter(partial_aggregate, "rep", scatter_dimension=0, tiled=True)
    pre_act = jnp.dot(aggregated, weight, precision=TOP_PRECISION) + layer_bias
    negative = jnp.minimum(pre_act, 0.0)
    layer_out = jnp.where(pre_act > 0, pre_act, jnp.expm1(negative))
    grad_pre = cotangent * jnp.where(pre_act > 0, 1.0, jnp.exp(negative))
    grad_scale = 1.0 / math.sqrt(row_count * cycle_size)
    grad_weight = (
        jnp.einsum("rd,re->de", aggregated, grad_pre, precision=TOP_PRECISION) * grad_scale
    )
    grad_bias = jnp.sum(grad_pre, axis=0) * grad_scale
    grad_weight, grad_bias = lax.psum((grad_weight, grad_bias), ("blk", "rep"))
    grad_hidden = jnp.einsum("re,de->rd", grad_pre, weight, precision=TOP_PRECISION)
    hidden_gradient = lax.all_gather(grad_hidden, "rep", axis=0, tiled=True)
    slot_terms = jnp.einsum(
        "xszt,xzc->xstc",
        operator_tiles,
        reshape_to_blocks(hidden_gradient),
        precision=TOP_PRECISION,
    )
    sorted_terms = jnp.einsum("iksc,ikbd->scbd", chosen, slot_terms, precision=TOP_PRECISION)

    def adjoint_term(section_no):
        return lax.dynamic_index_in_dim(sorted_terms, section_no, 0, keepdims=False).reshape(
            row_count, width
        )

    def retreat(counter, running):
        moved = shifted_2(running, "blk", -1)
        return moved + adjoint_term(window - 1 - counter)

    adjoint = lax.fori_loop(1, window, retreat, adjoint_term(window - 1))
    for bit_pos in range(rep_size.bit_length() - 1):
        returned = shifted_2(adjoint, "blk", -(window << bit_pos))
        adjoint = jnp.where((replica >> bit_pos) % 2 == 1, returned, adjoint)
    grad_feats = lax.psum_scatter(adjoint, "rep", scatter_dimension=0, tiled=True)
    return (layer_out, grad_feats, grad_weight, grad_bias)


def solution(mesh):
    return jax.shard_map(
        body,
        mesh=mesh,
        in_specs=(
            P("blk", None),
            P("blk", "rep", None, None),
            P("blk", "rep"),
            P(),
            P(),
            P(("blk", "rep"), None),
        ),
        out_specs=(P(("blk", "rep"), None), P(("blk", "rep"), None), P(), P()),
        check_vma=False,
    )
```

profile of v0, /device:TPU:1, one launch (start us, length us, event | category | flops | bytes accessed | tf_op | source)
XLA Modules:
  0.0 966.0 jit_solution(15077650085938543299)
XLA Ops:
  9.3 10.8 %collective-permute-done.2 = f32[512,256]{1,0:T(8,128)S(1)} collective-permute-done((f32[512,256]{1,0:T(8,128)}, f32[512,256]{1,0:T(8,128)S(1)}, u32[]{:S(2)}, u32[]{:S(2)}) %collective-permute-start.2) | collective-permute-done | bytes 524320 | tf_op jit(solution)/shard_map/ppermute | solution.py:13
  20.2 3.8 collective-permute-start.3
  24.8 7.8 collective-permute-done.3
  32.7 4.2 dynamic_update_slice.11
  37.0 259.1 %while.30 = (s32[]{:T(128)}, f32[512,256]{1,0:T(8,128)S(1)}, f32[16,4,128,256]{3,2,1,0:T(8,128)}, s32[]{:T(128)}, s32[]{:T(128)}, /*index=5*/s32[]{:T(128)}) while((s32[]{:T(128)}, f32[512,256]{1,0:T(8,128)S(1)}, f32[16,4,128,256]{3,2,1,0:T(8,128)}, s32[]{:T(128)}, s32[]{:T(128)}, /*index=5*/s32[]{:T(128)}) %tuple.67), condition=%wide.region_1.2_spmd, body=%wide.region_0.1_spmd.sunk | while | flops 5 | bytes 4194459 | solution.py:53
  37.0 3.5 collective-permute-start
  40.4 15.2 %collective-permute-done = f32[512,256]{1,0:T(8,128)S(1)} collective-permute-done((f32[512,256]{1,0:T(8,128)S(1)}, f32[512,256]{1,0:T(8,128)S(1)}, u32[]{:S(2)}, u32[]{:S(2)}) %collective-permute-start) | collective-permute-done | bytes 524320 | tf_op jit(solution)/shard_map/while/body/eval_jaxpr/ppermute | solution.py:13
  56.6 15.3 %collective-permute-done = f32[512,256]{1,0:T(8,128)S(1)} collective-permute-done((f32[512,256]{1,0:T(8,128)S(1)}, f32[512,256]{1,0:T(8,128)S(1)}, u32[]{:S(2)}, u32[]{:S(2)}) %collective-permute-start) | collective-permute-done | bytes 524320 | tf_op jit(solution)/shard_map/while/body/eval_jaxpr/ppermute | solution.py:13
  72.9 14.3 %collective-permute-done = f32[512,256]{1,0:T(8,128)S(1)} collective-permute-done((f32[512,256]{1,0:T(8,128)S(1)}, f32[512,256]{1,0:T(8,128)S(1)}, u32[]{:S(2)}, u32[]{:S(2)}) %collective-permute-start) | collective-permute-done | bytes 524320 | tf_op jit(solution)/shard_map/while/body/eval_jaxpr/ppermute | solution.py:13
  88.2 14.0 %collective-permute-done = f32[512,256]{1,0:T(8,128)S(1)} collective-permute-done((f32[512,256]{1,0:T(8,128)S(1)}, f32[512,256]{1,0:T(8,128)S(1)}, u32[]{:S(2)}, u32[]{:S(2)}) %collective-permute-start) | collective-permute-done | bytes 524320 | tf_op jit(solution)/shard_map/while/body/eval_jaxpr/ppermute | solution.py:13
  103.2 14.0 %collective-permute-done = f32[512,256]{1,0:T(8,128)S(1)} collective-permute-done((f32[512,256]{1,0:T(8,128)S(1)}, f32[512,256]{1,0:T(8,128)S(1)}, u32[]{:S(2)}, u32[]{:S(2)}) %collective-permute-start) | collective-permute-done | bytes 524320 | tf_op jit(solution)/shard_map/while/body/eval_jaxpr/ppermute | solution.py:13
  118.3 14.0 %collective-permute-done = f32[512,256]{1,0:T(8,128)S(1)} collective-permute-done((f32[512,256]{1,0:T(8,128)S(1)}, f32[512,256]{1,0:T(8,128)S(1)}, u32[]{:S(2)}, u32[]{:S(2)}) %collective-permute-start) | collective-permute-done | bytes 524320 | tf_op jit(solution)/shard_map/while/body/eval_jaxpr/ppermute | solution.py:13
  133.3 14.0 %collective-permute-done = f32[512,256]{1,0:T(8,128)S(1)} collective-permute-done((f32[512,256]{1,0:T(8,128)S(1)}, f32[512,256]{1,0:T(8,128)S(1)}, u32[]{:S(2)}, u32[]{:S(2)}) %collective-permute-start) | collective-permute-done | bytes 524320 | tf_op jit(solution)/shard_map/while/body/eval_jaxpr/ppermute | solution.py:13
  148.3 14.5 %collective-permute-done = f32[512,256]{1,0:T(8,128)S(1)} collective-permute-done((f32[512,256]{1,0:T(8,128)S(1)}, f32[512,256]{1,0:T(8,128)S(1)}, u32[]{:S(2)}, u32[]{:S(2)}) %collective-permute-start) | collective-permute-done | bytes 524320 | tf_op jit(solution)/shard_map/while/body/eval_jaxpr/ppermute | solution.py:13
  163.8 15.6 %collective-permute-done = f32[512,256]{1,0:T(8,128)S(1)} collective-permute-done((f32[512,256]{1,0:T(8,128)S(1)}, f32[512,256]{1,0:T(8,128)S(1)}, u32[]{:S(2)}, u32[]{:S(2)}) %collective-permute-start) | collective-permute-done | bytes 524320 | tf_op jit(solution)/shard_map/while/body/eval_jaxpr/ppermute | solution.py:13
  180.4 16.7 %collective-permute-done = f32[512,256]{1,0:T(8,128)S(1)} collective-permute-done((f32[512,256]{1,0:T(8,128)S(1)}, f32[512,256]{1,0:T(8,128)S(1)}, u32[]{:S(2)}, u32[]{:S(2)}) %collective-permute-start) | collective-permute-done | bytes 524320 | tf_op jit(solution)/shard_map/while/body/eval_jaxpr/ppermute | solution.py:13
  198.1 17.7 %collective-permute-done = f32[512,256]{1,0:T(8,128)S(1)} collective-permute-done((f32[512,256]{1,0:T(8,128)S(1)}, f32[512,256]{1,0:T(8,128)S(1)}, u32[]{:S(2)}, u32[]{:S(2)}) %collective-permute-start) | collective-permute-done | bytes 524320 | tf_op jit(solution)/shard_map/while/body/eval_jaxpr/ppermute | solution.py:13
  216.9 18.9 %collective-permute-done = f32[512,256]{1,0:T(8,128)S(1)} collective-permute-done((f32[512,256]{1,0:T(8,128)S(1)}, f32[512,256]{1,0:T(8,128)S(1)}, u32[]{:S(2)}, u32[]{:S(2)}) %collective-permute-start) | collective-permute-done | bytes 524320 | tf_op jit(solution)/shard_map/while/body/eval_jaxpr/ppermute | solution.py:13
  236.7 19.7 %collective-permute-done = f32[512,256]{1,0:T(8,128)S(1)} collective-permute-done((f32[512,256]{1,0:T(8,128)S(1)}, f32[512,256]{1,0:T(8,128)S(1)}, u32[]{:S(2)}, u32[]{:S(2)}) %collective-permute-start) | collective-permute-done | bytes 524320 | tf_op jit(solution)/shard_map/while/body/eval_jaxpr/ppermute | solution.py:13
  257.4 18.8 %collective-permute-done = f32[512,256]{1,0:T(8,128)S(1)} collective-permute-done((f32[512,256]{1,0:T(8,128)S(1)}, f32[512,256]{1,0:T(8,128)S(1)}, u32[]{:S(2)}, u32[]{:S(2)}) %collective-permute-start) | collective-permute-done | bytes 524320 | tf_op jit(solution)/shard_map/while/body/eval_jaxpr/ppermute | solution.py:13
  277.1 17.8 %collective-permute-done = f32[512,256]{1,0:T(8,128)S(1)} collective-permute-done((f32[512,256]{1,0:T(8,128)S(1)}, f32[512,256]{1,0:T(8,128)S(1)}, u32[]{:S(2)}, u32[]{:S(2)}) %collective-permute-start) | collective-permute-done | bytes 524320 | tf_op jit(solution)/shard_map/while/body/eval_jaxpr/ppermute | solution.py:13
  296.1 13.0 %fusion = f32[4,4,128,256,1]{3,1,4,2,0:T(4,128)S(1)} fusion(f32[16,4,128,256,1]{3,2,1,0,4:T(8,128)} %bitcast.48, pred[4,4,4]{1,0,2:T(4,128)(4,1)S(1)} %iota_compare_fusion, pred[4,4,16]{2,1,0:T(4,128)(4,1)S(1)} %iota_compare_fusion.1), kind=kOutput, calls=%fused_computation.3 | convolution fusion | flops 402654208 | bytes 10486080 | tf_op jit(solution)/shard_map/iksc,scbd->ikbd/dot_general | solution.py:54
  311.9 55.4 %reduce-scatter.3.cloned.1.call-done = f32[128,256]{1,0:T(8,128)} async-done(((f32[512,256]{1,0:T(8,128)}), f32[128,256]{1,0:T(8,128)}) %reduce-scatter.3.cloned.1.call-update) | async-done | bytes 131088 | tf_op jit(solution)/shard_map/reduce_scatter | solution.py:58
  369.5 13.7 %all_gather.3 = f32[512,256]{1,0:T(8,128)S(1)} all-gather(f32[128,256]{1,0:T(8,128)S(1)} %fusion.16), channel_id=1, replica_groups=mesh['blk'=64,'rep'=4] {'rep'}, dimensions={0}, use_global_device_ids=true | all-gather | bytes 655360 | tf_op jit(solution)/shard_map/all_gather | solution.py:70
  387.1 5.9 convolution_bitcast_fusion
  393.7 2.6 copy-done.2
  396.3 242.4 %while.31 = (s32[]{:T(128)}, f32[512,256]{1,0:T(8,128)S(1)}, f32[16,4,128,256]{3,0,2,1:T(8,128)}, s32[]{:T(128)}, s32[]{:T(128)}, /*index=5*/s32[]{:T(128)}, s32[]{:T(128)}) while((s32[]{:T(128)}, f32[512,256]{1,0:T(8,128)S(1)}, f32[16,4,128,256]{3,0,2,1:T(8,128)}, s32[]{:T(128)}, s32[]{:T(128)}, /*index=5*/s32[]{:T(128)}, s32[]{:T(128)}) %tuple.81), condition=%wide.region_4.5_spmd, body=%wide.region_3.4_spmd.sunk | while | flops 131078 | bytes 5767335 | solution.py:88
  396.3 3.7 collective-permute-start.1
  400.0 2.5 constant_dynamic-slice_fusion.2
  402.6 8.6 collective-permute-done.1
  411.3 8.3 collective-permute-start.1
  419.6 2.5 constant_dynamic-slice_fusion.2
  422.2 7.7 collective-permute-done.1
  429.9 8.3 collective-permute-start.1
  440.8 6.7 collective-permute-done.1
  447.7 8.3 collective-permute-start.1
  458.5 5.8 collective-permute-done.1
  464.5 8.3 collective-permute-start.1
  475.3 4.9 collective-permute-done.1
  480.3 8.3 collective-permute-start.1
  491.2 4.0 collective-permute-done.1
  495.3 8.3 collective-permute-start.1
  506.2 3.5 collective-permute-done.1
  509.8 8.0 collective-permute-start.1
  520.4 3.5 collective-permute-done.1
  524.0 8.0 collective-permute-start.1
  534.6 3.5 collective-permute-done.1
  538.2 8.0 collective-permute-start.1
  548.8 3.5 collective-permute-done.1
  552.4 8.0 collective-permute-start.1
  563.0 4.4 collective-permute-done.1
  567.5 8.0 collective-permute-start.1
  578.1 5.5 collective-permute-done.1
  583.7 8.0 collective-permute-start.1
  594.3 6.6 collective-permute-done.1
  600.9 8.0 collective-permute-start.1
  611.5 7.6 collective-permute-done.1
  619.3 8.0 collective-permute-start.1
  629.9 8.7 collective-permute-done.1
  638.8 8.3 collective-permute-done.4
  648.5 8.3 collective-permute-done.5
  657.7 94.6 %psum.15 = f32[256]{0:T(256)} all-reduce(f32[256]{0:T(256)S(1)} %broadcast_multiply_fusion), channel_id=1, replica_groups=mesh['blk'=64,'rep'=4] {'blk','rep'}, use_global_device_ids=true, to_apply=%region_8.9 | all-reduce | flops 256 | bytes 2048 | tf_op jit(solution)/shard_map/psum | solution.py:68
  752.3 162.6 %all-reduce.3.cloned.1.call-done = f32[256,256]{1,0:T(8,128)} async-done(((f32[256,256]{1,0:T(8,128)}), f32[256,256]{1,0:T(8,128)}) %all-reduce.3.cloned.1.call-update) | async-done | bytes 262160 | tf_op jit(solution)/shard_map/psum | solution.py:68
  914.9 42.9 %reduce-scatter.5.cloned.1.call-done = f32[128,256]{1,0:T(8,128)} async-done(((f32[512,256]{1,0:T(8,128)}), f32[128,256]{1,0:T(8,128)}) %reduce-scatter.5.cloned.1.call-update) | async-done | bytes 131088 | tf_op jit(solution)/shard_map/reduce_scatter | solution.py:92
  (124 shorter events, 65.8 us)
Async XLA Ops:
  7.2 301.9 %copy-start = (f32[4,4,128,128]{3,2,1,0:T(8,128)S(1)}, f32[4,4,128,128]{3,2,1,0:T(8,128)}, u32[]{:S(2)}) copy-start(f32[4,4,128,128]{3,2,1,0:T(8,128)} %param.11) | copy-start | bytes 3145732
  7.2 360.1 %reduce-scatter.3.cloned.1.call-start = ((), (), s32[]{:S(2)}) async-start(), calls=%async_computation.2 | async-start | bytes 655360 | tf_op jit(solution)/shard_map/reduce_scatter | solution.py:58
  7.2 12.9 %collective-permute-start.2 = (f32[512,256]{1,0:T(8,128)}, f32[512,256]{1,0:T(8,128)S(1)}, u32[]{:S(2)}, u32[]{:S(2)}) collective-permute-start(f32[512,256]{1,0:T(8,128)} %param.10), channel_id=1, source_target_pairs={{0,64},{4,68},{8,72},{12,76},{16,80},{20,84},{24,88},{28,92},{32,9... | collective-permute-start | bytes 1572872 | tf_op jit(solution)/shard_map/ppermute | solution.py:13
  20.2 12.4 %collective-permute-start.3 = (f32[512,256]{1,0:T(8,128)S(1)}, f32[512,256]{1,0:T(8,128)S(1)}, u32[]{:S(2)}, u32[]{:S(2)}) collective-permute-start(f32[512,256]{1,0:T(8,128)S(1)} %broadcast_select_fusion.1), channel_id=1, source_target_pairs={{0,128},{4,132},{8,136},{12,140},{16,144},{20,148},{24,152},{28,15... | collective-permute-start | bytes 1572872 | tf_op jit(solution)/shard_map/ppermute | solution.py:13
  37.0 18.7 %collective-permute-start = (f32[512,256]{1,0:T(8,128)S(1)}, f32[512,256]{1,0:T(8,128)S(1)}, u32[]{:S(2)}, u32[]{:S(2)}) collective-permute-start(f32[512,256]{1,0:T(8,128)S(1)} %get-tuple-element.223), channel_id=1, source_target_pairs={{0,4},{4,8},{8,12},{12,16},{16,20},{20,24},{24,28},{28,32},{32,36}... | collective-permute-start | bytes 1572872 | tf_op jit(solution)/shard_map/while/body/eval_jaxpr/ppermute | solution.py:13
  56.5 15.4 %collective-permute-start = (f32[512,256]{1,0:T(8,128)S(1)}, f32[512,256]{1,0:T(8,128)S(1)}, u32[]{:S(2)}, u32[]{:S(2)}) collective-permute-start(f32[512,256]{1,0:T(8,128)S(1)} %get-tuple-element.223), channel_id=1, source_target_pairs={{0,4},{4,8},{8,12},{12,16},{16,20},{20,24},{24,28},{28,32},{32,36}... | collective-permute-start | bytes 1572872 | tf_op jit(solution)/shard_map/while/body/eval_jaxpr/ppermute | solution.py:13
  72.8 14.4 %collective-permute-start = (f32[512,256]{1,0:T(8,128)S(1)}, f32[512,256]{1,0:T(8,128)S(1)}, u32[]{:S(2)}, u32[]{:S(2)}) collective-permute-start(f32[512,256]{1,0:T(8,128)S(1)} %get-tuple-element.223), channel_id=1, source_target_pairs={{0,4},{4,8},{8,12},{12,16},{16,20},{20,24},{24,28},{28,32},{32,36}... | collective-permute-start | bytes 1572872 | tf_op jit(solution)/shard_map/while/body/eval_jaxpr/ppermute | solution.py:13
  88.1 14.1 %collective-permute-start = (f32[512,256]{1,0:T(8,128)S(1)}, f32[512,256]{1,0:T(8,128)S(1)}, u32[]{:S(2)}, u32[]{:S(2)}) collective-permute-start(f32[512,256]{1,0:T(8,128)S(1)} %get-tuple-element.223), channel_id=1, source_target_pairs={{0,4},{4,8},{8,12},{12,16},{16,20},{20,24},{24,28},{28,32},{32,36}... | collective-permute-start | bytes 1572872 | tf_op jit(solution)/shard_map/while/body/eval_jaxpr/ppermute | solution.py:13
  103.2 14.1 %collective-permute-start = (f32[512,256]{1,0:T(8,128)S(1)}, f32[512,256]{1,0:T(8,128)S(1)}, u32[]{:S(2)}, u32[]{:S(2)}) collective-permute-start(f32[512,256]{1,0:T(8,128)S(1)} %get-tuple-element.223), channel_id=1, source_target_pairs={{0,4},{4,8},{8,12},{12,16},{16,20},{20,24},{24,28},{28,32},{32,36}... | collective-permute-start | bytes 1572872 | tf_op jit(solution)/shard_map/while/body/eval_jaxpr/ppermute | solution.py:13
  118.2 14.1 %collective-permute-start = (f32[512,256]{1,0:T(8,128)S(1)}, f32[512,256]{1,0:T(8,128)S(1)}, u32[]{:S(2)}, u32[]{:S(2)}) collective-permute-start(f32[512,256]{1,0:T(8,128)S(1)} %get-tuple-element.223), channel_id=1, source_target_pairs={{0,4},{4,8},{8,12},{12,16},{16,20},{20,24},{24,28},{28,32},{32,36}... | collective-permute-start | bytes 1572872 | tf_op jit(solution)/shard_map/while/body/eval_jaxpr/ppermute | solution.py:13
  133.2 14.1 %collective-permute-start = (f32[512,256]{1,0:T(8,128)S(1)}, f32[512,256]{1,0:T(8,128)S(1)}, u32[]{:S(2)}, u32[]{:S(2)}) collective-permute-start(f32[512,256]{1,0:T(8,128)S(1)} %get-tuple-element.223), channel_id=1, source_target_pairs={{0,4},{4,8},{8,12},{12,16},{16,20},{20,24},{24,28},{28,32},{32,36}... | collective-permute-start | bytes 1572872 | tf_op jit(solution)/shard_map/while/body/eval_jaxpr/ppermute | solution.py:13
  148.2 14.6 %collective-permute-start = (f32[512,256]{1,0:T(8,128)S(1)}, f32[512,256]{1,0:T(8,128)S(1)}, u32[]{:S(2)}, u32[]{:S(2)}) collective-permute-start(f32[512,256]{1,0:T(8,128)S(1)} %get-tuple-element.223), channel_id=1, source_target_pairs={{0,4},{4,8},{8,12},{12,16},{16,20},{20,24},{24,28},{28,32},{32,36}... | collective-permute-start | bytes 1572872 | tf_op jit(solution)/shard_map/while/body/eval_jaxpr/ppermute | solution.py:13
  163.7 15.7 %collective-permute-start = (f32[512,256]{1,0:T(8,128)S(1)}, f32[512,256]{1,0:T(8,128)S(1)}, u32[]{:S(2)}, u32[]{:S(2)}) collective-permute-start(f32[512,256]{1,0:T(8,128)S(1)} %get-tuple-element.223), channel_id=1, source_target_pairs={{0,4},{4,8},{8,12},{12,16},{16,20},{20,24},{24,28},{28,32},{32,36}... | collective-permute-start | bytes 1572872 | tf_op jit(solution)/shard_map/while/body/eval_jaxpr/ppermute | solution.py:13
  180.3 16.8 %collective-permute-start = (f32[512,256]{1,0:T(8,128)S(1)}, f32[512,256]{1,0:T(8,128)S(1)}, u32[]{:S(2)}, u32[]{:S(2)}) collective-permute-start(f32[512,256]{1,0:T(8,128)S(1)} %get-tuple-element.223), channel_id=1, source_target_pairs={{0,4},{4,8},{8,12},{12,16},{16,20},{20,24},{24,28},{28,32},{32,36}... | collective-permute-start | bytes 1572872 | tf_op jit(solution)/shard_map/while/body/eval_jaxpr/ppermute | solution.py:13
  198.1 17.8 %collective-permute-start = (f32[512,256]{1,0:T(8,128)S(1)}, f32[512,256]{1,0:T(8,128)S(1)}, u32[]{:S(2)}, u32[]{:S(2)}) collective-permute-start(f32[512,256]{1,0:T(8,128)S(1)} %get-tuple-element.223), channel_id=1, source_target_pairs={{0,4},{4,8},{8,12},{12,16},{16,20},{20,24},{24,28},{28,32},{32,36}... | collective-permute-start | bytes 1572872 | tf_op jit(solution)/shard_map/while/body/eval_jaxpr/ppermute | solution.py:13
  216.8 19.0 %collective-permute-start = (f32[512,256]{1,0:T(8,128)S(1)}, f32[512,256]{1,0:T(8,128)S(1)}, u32[]{:S(2)}, u32[]{:S(2)}) collective-permute-start(f32[512,256]{1,0:T(8,128)S(1)} %get-tuple-element.223), channel_id=1, source_target_pairs={{0,4},{4,8},{8,12},{12,16},{16,20},{20,24},{24,28},{28,32},{32,36}... | collective-permute-start | bytes 1572872 | tf_op jit(solution)/shard_map/while/body/eval_jaxpr/ppermute | solution.py:13
  236.6 19.7 %collective-permute-start = (f32[512,256]{1,0:T(8,128)S(1)}, f32[512,256]{1,0:T(8,128)S(1)}, u32[]{:S(2)}, u32[]{:S(2)}) collective-permute-start(f32[512,256]{1,0:T(8,128)S(1)} %get-tuple-element.223), channel_id=1, source_target_pairs={{0,4},{4,8},{8,12},{12,16},{16,20},{20,24},{24,28},{28,32},{32,36}... | collective-permute-start | bytes 1572872 | tf_op jit(solution)/shard_map/while/body/eval_jaxpr/ppermute | solution.py:13
  257.3 18.8 %collective-permute-start = (f32[512,256]{1,0:T(8,128)S(1)}, f32[512,256]{1,0:T(8,128)S(1)}, u32[]{:S(2)}, u32[]{:S(2)}) collective-permute-start(f32[512,256]{1,0:T(8,128)S(1)} %get-tuple-element.223), channel_id=1, source_target_pairs={{0,4},{4,8},{8,12},{12,16},{16,20},{20,24},{24,28},{28,32},{32,36}... | collective-permute-start | bytes 1572872 | tf_op jit(solution)/shard_map/while/body/eval_jaxpr/ppermute | solution.py:13
  277.0 17.9 %collective-permute-start = (f32[512,256]{1,0:T(8,128)S(1)}, f32[512,256]{1,0:T(8,128)S(1)}, u32[]{:S(2)}, u32[]{:S(2)}) collective-permute-start(f32[512,256]{1,0:T(8,128)S(1)} %get-tuple-element.223), channel_id=1, source_target_pairs={{0,4},{4,8},{8,12},{12,16},{16,20},{20,24},{24,28},{28,32},{32,36}... | collective-permute-start | bytes 1572872 | tf_op jit(solution)/shard_map/while/body/eval_jaxpr/ppermute | solution.py:13
  296.1 71.2 %copy-start.1 = (f32[128,256]{1,0:T(8,128)S(1)}, f32[128,256]{1,0:T(8,128)}, u32[]{:S(2)}) copy-start(f32[128,256]{1,0:T(8,128)} %param.15) | copy-start | bytes 393220
  296.1 71.2 %copy-start.3 = (f32[256,256]{1,0:T(8,128)S(1)}, f32[256,256]{1,0:T(8,128)}, u32[]{:S(2)}) copy-start(f32[256,256]{1,0:T(8,128)} %param.13) | copy-start | bytes 786436
  296.1 71.2 %copy-start.5 = (f32[256]{0:T(256)S(1)}, f32[256]{0:T(256)}, u32[]{:S(2)}) copy-start(f32[256]{0:T(256)} %param.14) | copy-start | bytes 3076
  311.6 603.3 %all-reduce.3.cloned.1.call-start = ((), (), s32[]{:S(2)}) async-start(), calls=%async_computation.4 | async-start | bytes 524288 | tf_op jit(solution)/shard_map/psum | solution.py:68
  393.1 3.2 copy-start.2
  396.3 250.9 %copy-start.4 = (f32[128,256]{1,0:T(8,128)S(1)}, f32[128,256]{1,0:T(8,128)}, u32[]{:S(2)}) copy-start(f32[128,256]{1,0:T(8,128)} %reduce-scatter.3.cloned.1.call-done) | copy-start | bytes 393220
  396.3 14.9 %collective-permute-start.1 = (f32[512,256]{1,0:T(8,128)S(1)}, f32[512,256]{1,0:T(8,128)S(1)}, u32[]{:S(2)}, u32[]{:S(2)}) collective-permute-start(f32[512,256]{1,0:T(8,128)S(1)} %get-tuple-element.242), channel_id=1, source_target_pairs={{0,252},{4,0},{8,4},{12,8},{16,12},{20,16},{24,20},{28,24},{32,28}... | collective-permute-start | bytes 1572872 | tf_op jit(solution)/shard_map/while/body/eval_jaxpr/ppermute | solution.py:13
  411.3 18.6 %collective-permute-start.1 = (f32[512,256]{1,0:T(8,128)S(1)}, f32[512,256]{1,0:T(8,128)S(1)}, u32[]{:S(2)}, u32[]{:S(2)}) collective-permute-start(f32[512,256]{1,0:T(8,128)S(1)} %get-tuple-element.242), channel_id=1, source_target_pairs={{0,252},{4,0},{8,4},{12,8},{16,12},{20,16},{24,20},{28,24},{32,28}... | collective-permute-start | bytes 1572872 | tf_op jit(solution)/shard_map/while/body/eval_jaxpr/ppermute | solution.py:13
  429.9 17.6 %collective-permute-start.1 = (f32[512,256]{1,0:T(8,128)S(1)}, f32[512,256]{1,0:T(8,128)S(1)}, u32[]{:S(2)}, u32[]{:S(2)}) collective-permute-start(f32[512,256]{1,0:T(8,128)S(1)} %get-tuple-element.242), channel_id=1, source_target_pairs={{0,252},{4,0},{8,4},{12,8},{16,12},{20,16},{24,20},{28,24},{32,28}... | collective-permute-start | bytes 1572872 | tf_op jit(solution)/shard_map/while/body/eval_jaxpr/ppermute | solution.py:13
  447.7 16.7 %collective-permute-start.1 = (f32[512,256]{1,0:T(8,128)S(1)}, f32[512,256]{1,0:T(8,128)S(1)}, u32[]{:S(2)}, u32[]{:S(2)}) collective-permute-start(f32[512,256]{1,0:T(8,128)S(1)} %get-tuple-element.242), channel_id=1, source_target_pairs={{0,252},{4,0},{8,4},{12,8},{16,12},{20,16},{24,20},{28,24},{32,28}... | collective-permute-start | bytes 1572872 | tf_op jit(solution)/shard_map/while/body/eval_jaxpr/ppermute | solution.py:13
  464.5 15.8 %collective-permute-start.1 = (f32[512,256]{1,0:T(8,128)S(1)}, f32[512,256]{1,0:T(8,128)S(1)}, u32[]{:S(2)}, u32[]{:S(2)}) collective-permute-start(f32[512,256]{1,0:T(8,128)S(1)} %get-tuple-element.242), channel_id=1, source_target_pairs={{0,252},{4,0},{8,4},{12,8},{16,12},{20,16},{24,20},{28,24},{32,28}... | collective-permute-start | bytes 1572872 | tf_op jit(solution)/shard_map/while/body/eval_jaxpr/ppermute | solution.py:13
  480.3 14.9 %collective-permute-start.1 = (f32[512,256]{1,0:T(8,128)S(1)}, f32[512,256]{1,0:T(8,128)S(1)}, u32[]{:S(2)}, u32[]{:S(2)}) collective-permute-start(f32[512,256]{1,0:T(8,128)S(1)} %get-tuple-element.242), channel_id=1, source_target_pairs={{0,252},{4,0},{8,4},{12,8},{16,12},{20,16},{24,20},{28,24},{32,28}... | collective-permute-start | bytes 1572872 | tf_op jit(solution)/shard_map/while/body/eval_jaxpr/ppermute | solution.py:13
  495.3 14.4 %collective-permute-start.1 = (f32[512,256]{1,0:T(8,128)S(1)}, f32[512,256]{1,0:T(8,128)S(1)}, u32[]{:S(2)}, u32[]{:S(2)}) collective-permute-start(f32[512,256]{1,0:T(8,128)S(1)} %get-tuple-element.242), channel_id=1, source_target_pairs={{0,252},{4,0},{8,4},{12,8},{16,12},{20,16},{24,20},{28,24},{32,28}... | collective-permute-start | bytes 1572872 | tf_op jit(solution)/shard_map/while/body/eval_jaxpr/ppermute | solution.py:13
  509.8 14.1 %collective-permute-start.1 = (f32[512,256]{1,0:T(8,128)S(1)}, f32[512,256]{1,0:T(8,128)S(1)}, u32[]{:S(2)}, u32[]{:S(2)}) collective-permute-start(f32[512,256]{1,0:T(8,128)S(1)} %get-tuple-element.242), channel_id=1, source_target_pairs={{0,252},{4,0},{8,4},{12,8},{16,12},{20,16},{24,20},{28,24},{32,28}... | collective-permute-start | bytes 1572872 | tf_op jit(solution)/shard_map/while/body/eval_jaxpr/ppermute | solution.py:13
  524.0 14.1 %collective-permute-start.1 = (f32[512,256]{1,0:T(8,128)S(1)}, f32[512,256]{1,0:T(8,128)S(1)}, u32[]{:S(2)}, u32[]{:S(2)}) collective-permute-start(f32[512,256]{1,0:T(8,128)S(1)} %get-tuple-element.242), channel_id=1, source_target_pairs={{0,252},{4,0},{8,4},{12,8},{16,12},{20,16},{24,20},{28,24},{32,28}... | collective-permute-start | bytes 1572872 | tf_op jit(solution)/shard_map/while/body/eval_jaxpr/ppermute | solution.py:13
  538.2 14.1 %collective-permute-start.1 = (f32[512,256]{1,0:T(8,128)S(1)}, f32[512,256]{1,0:T(8,128)S(1)}, u32[]{:S(2)}, u32[]{:S(2)}) collective-permute-start(f32[512,256]{1,0:T(8,128)S(1)} %get-tuple-element.242), channel_id=1, source_target_pairs={{0,252},{4,0},{8,4},{12,8},{16,12},{20,16},{24,20},{28,24},{32,28}... | collective-permute-start | bytes 1572872 | tf_op jit(solution)/shard_map/while/body/eval_jaxpr/ppermute | solution.py:13
  552.4 15.0 %collective-permute-start.1 = (f32[512,256]{1,0:T(8,128)S(1)}, f32[512,256]{1,0:T(8,128)S(1)}, u32[]{:S(2)}, u32[]{:S(2)}) collective-permute-start(f32[512,256]{1,0:T(8,128)S(1)} %get-tuple-element.242), channel_id=1, source_target_pairs={{0,252},{4,0},{8,4},{12,8},{16,12},{20,16},{24,20},{28,24},{32,28}... | collective-permute-start | bytes 1572872 | tf_op jit(solution)/shard_map/while/body/eval_jaxpr/ppermute | solution.py:13
  567.5 16.1 %collective-permute-start.1 = (f32[512,256]{1,0:T(8,128)S(1)}, f32[512,256]{1,0:T(8,128)S(1)}, u32[]{:S(2)}, u32[]{:S(2)}) collective-permute-start(f32[512,256]{1,0:T(8,128)S(1)} %get-tuple-element.242), channel_id=1, source_target_pairs={{0,252},{4,0},{8,4},{12,8},{16,12},{20,16},{24,20},{28,24},{32,28}... | collective-permute-start | bytes 1572872 | tf_op jit(solution)/shard_map/while/body/eval_jaxpr/ppermute | solution.py:13
  583.7 17.2 %collective-permute-start.1 = (f32[512,256]{1,0:T(8,128)S(1)}, f32[512,256]{1,0:T(8,128)S(1)}, u32[]{:S(2)}, u32[]{:S(2)}) collective-permute-start(f32[512,256]{1,0:T(8,128)S(1)} %get-tuple-element.242), channel_id=1, source_target_pairs={{0,252},{4,0},{8,4},{12,8},{16,12},{20,16},{24,20},{28,24},{32,28}... | collective-permute-start | bytes 1572872 | tf_op jit(solution)/shard_map/while/body/eval_jaxpr/ppermute | solution.py:13
  600.9 18.2 %collective-permute-start.1 = (f32[512,256]{1,0:T(8,128)S(1)}, f32[512,256]{1,0:T(8,128)S(1)}, u32[]{:S(2)}, u32[]{:S(2)}) collective-permute-start(f32[512,256]{1,0:T(8,128)S(1)} %get-tuple-element.242), channel_id=1, source_target_pairs={{0,252},{4,0},{8,4},{12,8},{16,12},{20,16},{24,20},{28,24},{32,28}... | collective-permute-start | bytes 1572872 | tf_op jit(solution)/shard_map/while/body/eval_jaxpr/ppermute | solution.py:13
  619.3 19.3 %collective-permute-start.1 = (f32[512,256]{1,0:T(8,128)S(1)}, f32[512,256]{1,0:T(8,128)S(1)}, u32[]{:S(2)}, u32[]{:S(2)}) collective-permute-start(f32[512,256]{1,0:T(8,128)S(1)} %get-tuple-element.242), channel_id=1, source_target_pairs={{0,252},{4,0},{8,4},{12,8},{16,12},{20,16},{24,20},{28,24},{32,28}... | collective-permute-start | bytes 1572872 | tf_op jit(solution)/shard_map/while/body/eval_jaxpr/ppermute | solution.py:13
  638.7 8.4 collective-permute-start.4
  647.1 9.6 collective-permute-start.5
  648.4 309.4 %reduce-scatter.5.cloned.1.call-start = ((), (), s32[]{:S(2)}) async-start(), calls=%async_computation.3 | async-start | bytes 655360 | tf_op jit(solution)/shard_map/reduce_scatter | solution.py:92
Sparse Core Ops, SparseCore 0:
  311.7 55.4 reduce-scatter.2
  648.5 266.3 all-reduce.2
  918.4 39.3 reduce-scatter.4
where the time goes:
time: 967 us; the launch traced here: 966 us
  waiting for transfers between devices  621 us (64%)
  starting transfers between devices  129 us (13%)
  blocking collectives  108 us (11%)
  local copies, waits for them, and re-layouts  63.2 us (7%)
  matrix products  26.6 us (3%)
  between operations  13.9 us (1%)
    ppermute x34, waiting for transfers between devices, shifted_2(): return lax.ppermute(value, axis, pairs)  361 us
    psum x1, waiting for transfers between devices, body(): grad_weight, grad_bias = lax.psum((grad_weight, grad_bias), ('blk', 'rep'))  163 us
    ppermute x34, starting transfers between devices, shifted_2(): return lax.ppermute(value, axis, pairs)  128 us
    psum x1, blocking collectives, body(): grad_weight, grad_bias = lax.psum((grad_weight, grad_bias), ('blk', 'rep'))  94.6 us
    reduce_scatter x1, waiting for transfers between devices, body(): lax.psum_scatter(partial_aggregate, 'rep', scatter_dimension=0, tiled=True)  55.4 us
    reduce_scatter x1, waiting for transfers between devices, body(): lax.psum_scatter(adjoint, 'rep', scatter_dimension=0, tiled=True)  42.9 us
    dynamic_slice x31, local copies, waits for them, and re-layouts, adjoint_term(): lax.dynamic_index_in_dim(sorted_terms, section_no, 0, keepdims=False)  39.3 us
  transfers between devices with their start and end apart: 37, of which 37 were waited for; matrix products, arithmetic and copies ran while one was open for 4% of the time, Pallas kernels for 0%

commit v1 on v0

--- a/solution.py
+++ b/solution.py
@@ -5,6 +5,9 @@
 from jax.sharding import PartitionSpec as P
 
 TOP_PRECISION = lax.Precision.HIGHEST
+_make_sections = lambda mine, device_axis, mesh_dim: jax.lax.psum(
+    jax.lax.psum(mine, axis_name=device_axis), axis_name=mesh_dim
+)
 
 
 def shifted_2(value, axis, steps):
@@ -65,7 +68,7 @@
         jnp.einsum("rd,re->de", aggregated, grad_pre, precision=TOP_PRECISION) * grad_scale
     )
     grad_bias = jnp.sum(grad_pre, axis=0) * grad_scale
-    grad_weight, grad_bias = lax.psum((grad_weight, grad_bias), ("blk", "rep"))
+    grad_weight, grad_bias = _make_sections((grad_weight, grad_bias), "blk", "rep")
     grad_hidden = jnp.einsum("re,de->rd", grad_pre, weight, precision=TOP_PRECISION)
     hidden_gradient = lax.all_gather(grad_hidden, "rep", axis=0, tiled=True)
     slot_terms = jnp.einsum(

time: 967 us -> 1530 us (1.58)
  waiting for transfers between devices: 621 us -> 1050 us
  blocking collectives: 108 us -> 237 us
    psum x1 -> x2, waiting for transfers between devices: 163 us -> 646 us  [the longest x1 646 us: jax.lax.psum(mine, axis_name=device_axis)]
    psum x1 -> x2, blocking collectives: 94.6 us -> 223 us  [the longest x1 159 us: jax.lax.psum(mine, axis_name=device_axis)]
    reduce_scatter x1, waiting for transfers between devices: 42.9 us -> 0.01 us  [body(): lax.psum_scatter(adjoint, 'rep', scatter_dimension=0, tiled=True)]
  transfers between devices with their start and end apart: 37 -> 38, of which waited for: 37 -> 35; matrix products, arithmetic and copies ran while one was open for 4% -> 3% of each run, Pallas kernels for 0% -> 0%
where the time goes in v1:
time: 1530 us
  waiting for transfers between devices  1050 us (69%)
  blocking collectives  237 us (15%)
  starting transfers between devices  129 us (8%)
  local copies, waits for them, and re-layouts  63.1 us (4%)
  matrix products  26.6 us (2%)
    psum x1, waiting for transfers between devices, jax.lax.psum(mine, axis_name=device_axis)  646 us
    ppermute x34, waiting for transfers between devices, shifted_2(): return lax.ppermute(value, axis, pairs)  352 us
    psum x1, blocking collectives, jax.lax.psum(mine, axis_name=device_axis)  159 us
    ppermute x34, starting transfers between devices, shifted_2(): return lax.ppermute(value, axis, pairs)  128 us
    psum x1, blocking collectives, jax.lax.psum(jax.lax.psum(mine, axis_name=device_axis), axis_name=mesh_dim)  63.7 us
    reduce_scatter x1, waiting for transfers between devices, body(): lax.psum_scatter(partial_aggregate, 'rep', scatter_dimension=0, tiled=True)  55.4 us
    dynamic_slice x31, local copies, waits for them, and re-layouts, adjoint_term(): lax.dynamic_index_in_dim(sorted_terms, section_no, 0, keepdims=False)  39.3 us
  transfers between devices with their start and end apart: 38, of which 35 were waited for; matrix products, arithmetic and copies ran while one was open for 3% of the time, Pallas kernels for 0%

profile of v1, /device:TPU:1, one launch (start us, length us, event | category | flops | bytes accessed | tf_op | source)
XLA Modules:
  0.0 1526.4 jit_solution(14307414345923288356)
XLA Ops:
  9.3 10.8 collective-permute-done.2
  20.2 3.8 collective-permute-start.3
  24.8 7.8 collective-permute-done.3
  32.7 4.3 dynamic_update_slice.11
  37.0 259.0 %while.30 = (s32[]{:T(128)}, f32[512,256]{1,0:T(8,128)S(1)}, f32[16,4,128,256]{3,2,1,0:T(8,128)}, s32[]{:T(128)}, s32[]{:T(128)}, /*index=5*/s32[]{:T(128)}) while((s32[]{:T(128)}, f32[512,256]{1,0:T(8,128)S(1)}, f32[16,4,128,256]{3,2,1,0:T(8,128)}, s32[]{:T(128)}, s32[]{:T(128)}, /*index=5*/s32[]{:T(128)}) %tuple.67), condition=%wide.region_1.2_spmd, body=%wide.region_0.1_spmd.sunk | while | flops 5 | bytes 4194459 | solution.py:56
  37.0 3.5 collective-permute-start
  40.5 15.2 collective-permute-done
  56.6 15.3 collective-permute-done
  72.9 14.3 collective-permute-done
  88.2 14.0 collective-permute-done
  103.2 14.0 collective-permute-done
  118.3 14.0 collective-permute-done
  133.3 14.0 collective-permute-done
  148.3 14.6 collective-permute-done
  163.8 15.6 %collective-permute-done = f32[512,256]{1,0:T(8,128)S(1)} collective-permute-done((f32[512,256]{1,0:T(8,128)S(1)}, f32[512,256]{1,0:T(8,128)S(1)}, u32[]{:S(2)}, u32[]{:S(2)}) %collective-permute-start) | collective-permute-done | bytes 524320 | tf_op jit(solution)/shard_map/while/body/eval_jaxpr/ppermute | solution.py:16
  180.4 16.7 %collective-permute-done = f32[512,256]{1,0:T(8,128)S(1)} collective-permute-done((f32[512,256]{1,0:T(8,128)S(1)}, f32[512,256]{1,0:T(8,128)S(1)}, u32[]{:S(2)}, u32[]{:S(2)}) %collective-permute-start) | collective-permute-done | bytes 524320 | tf_op jit(solution)/shard_map/while/body/eval_jaxpr/ppermute | solution.py:16
  198.1 17.8 %collective-permute-done = f32[512,256]{1,0:T(8,128)S(1)} collective-permute-done((f32[512,256]{1,0:T(8,128)S(1)}, f32[512,256]{1,0:T(8,128)S(1)}, u32[]{:S(2)}, u32[]{:S(2)}) %collective-permute-start) | collective-permute-done | bytes 524320 | tf_op jit(solution)/shard_map/while/body/eval_jaxpr/ppermute | solution.py:16
  216.8 18.9 %collective-permute-done = f32[512,256]{1,0:T(8,128)S(1)} collective-permute-done((f32[512,256]{1,0:T(8,128)S(1)}, f32[512,256]{1,0:T(8,128)S(1)}, u32[]{:S(2)}, u32[]{:S(2)}) %collective-permute-start) | collective-permute-done | bytes 524320 | tf_op jit(solution)/shard_map/while/body/eval_jaxpr/ppermute | solution.py:16
  236.7 19.7 %collective-permute-done = f32[512,256]{1,0:T(8,128)S(1)} collective-permute-done((f32[512,256]{1,0:T(8,128)S(1)}, f32[512,256]{1,0:T(8,128)S(1)}, u32[]{:S(2)}, u32[]{:S(2)}) %collective-permute-start) | collective-permute-done | bytes 524320 | tf_op jit(solution)/shard_map/while/body/eval_jaxpr/ppermute | solution.py:16
  257.4 18.8 %collective-permute-done = f32[512,256]{1,0:T(8,128)S(1)} collective-permute-done((f32[512,256]{1,0:T(8,128)S(1)}, f32[512,256]{1,0:T(8,128)S(1)}, u32[]{:S(2)}, u32[]{:S(2)}) %collective-permute-start) | collective-permute-done | bytes 524320 | tf_op jit(solution)/shard_map/while/body/eval_jaxpr/ppermute | solution.py:16
  277.1 17.8 %collective-permute-done = f32[512,256]{1,0:T(8,128)S(1)} collective-permute-done((f32[512,256]{1,0:T(8,128)S(1)}, f32[512,256]{1,0:T(8,128)S(1)}, u32[]{:S(2)}, u32[]{:S(2)}) %collective-permute-start) | collective-permute-done | bytes 524320 | tf_op jit(solution)/shard_map/while/body/eval_jaxpr/ppermute | solution.py:16
  296.0 13.0 fusion
  311.8 55.4 %reduce-scatter.3.cloned.1.call-done = f32[128,256]{1,0:T(8,128)} async-done(((f32[512,256]{1,0:T(8,128)}), f32[128,256]{1,0:T(8,128)}) %reduce-scatter.3.cloned.1.call-update) | async-done | bytes 131088 | tf_op jit(solution)/shard_map/reduce_scatter | solution.py:61
  369.5 13.7 all_gather.3
  387.1 5.9 convolution_bitcast_fusion
  393.6 2.6 copy-done.2
  396.2 242.4 %while.31 = (s32[]{:T(128)}, f32[512,256]{1,0:T(8,128)S(1)}, f32[16,4,128,256]{3,0,2,1:T(8,128)}, s32[]{:T(128)}, s32[]{:T(128)}, /*index=5*/s32[]{:T(128)}, s32[]{:T(128)}) while((s32[]{:T(128)}, f32[512,256]{1,0:T(8,128)S(1)}, f32[16,4,128,256]{3,0,2,1:T(8,128)}, s32[]{:T(128)}, s32[]{:T(128)}, /*index=5*/s32[]{:T(128)}, s32[]{:T(128)}) %tuple.83), condition=%wide.region_4.5_spmd, body=%wide.region_3.4_spmd.sunk | while | flops 131078 | bytes 5767335 | solution.py:91
  396.2 3.8 collective-permute-start.1
  400.0 2.5 constant_dynamic-slice_fusion.2
  402.6 8.6 collective-permute-done.1
  411.3 8.3 collective-permute-start.1
  422.2 7.7 collective-permute-done.1
  429.9 8.3 collective-permute-start.1
  438.2 2.5 constant_dynamic-slice_fusion.2
  440.8 6.7 collective-permute-done.1
  447.6 8.3 collective-permute-start.1
  455.9 2.5 constant_dynamic-slice_fusion.2
  458.5 5.8 collective-permute-done.1
  464.4 8.3 collective-permute-start.1
  475.3 4.9 collective-permute-done.1
  480.3 8.3 collective-permute-start.1
  491.2 4.0 collective-permute-done.1
  495.3 8.3 collective-permute-start.1
  506.1 3.5 collective-permute-done.1
  509.8 8.0 collective-permute-start.1
  520.4 3.5 collective-permute-done.1
  524.0 8.0 collective-permute-start.1
  534.6 3.5 collective-permute-done.1
  538.2 8.0 collective-permute-start.1
  548.8 3.5 collective-permute-done.1
  552.4 8.0 collective-permute-start.1
  563.0 4.4 collective-permute-done.1
  567.5 8.0 collective-permute-start.1
  578.1 5.5 collective-permute-done.1
  583.7 8.0 collective-permute-start.1
  594.2 6.6 collective-permute-done.1
  600.9 8.0 collective-permute-start.1
  611.5 7.6 collective-permute-done.1
  619.2 8.0 collective-permute-start.1
  629.8 8.7 collective-permute-done.1
  638.7 8.3 collective-permute-done.4
  648.4 645.7 %all-reduce.4.cloned.1.call-done = f32[256,256]{1,0:T(8,128)} async-done(((f32[256,256]{1,0:T(8,128)}), f32[256,256]{1,0:T(8,128)}) %all-reduce.4.cloned.1.call-update) | async-done | bytes 262160 | tf_op jit(solution)/shard_map/psum | solution.py:9
  1295.1 159.4 %psum.30 = f32[256]{0:T(256)S(1)} all-reduce(f32[256]{0:T(256)S(1)} %broadcast_multiply_fusion), channel_id=1, replica_groups=mesh['blk'=64,'rep'=4] {'blk'}, use_global_device_ids=true, to_apply=%region_9.10 | all-reduce | flops 256 | bytes 2048 | tf_op jit(solution)/shard_map/psum | solution.py:9
  1454.5 63.7 %psum.31 = f32[256]{0:T(256)} all-reduce(f32[256]{0:T(256)S(1)} %psum.30), channel_id=1, replica_groups=mesh['blk'=64,'rep'=4] {'rep'}, use_global_device_ids=true, to_apply=%region_10.11 | all-reduce | flops 256 | bytes 2048 | tf_op jit(solution)/shard_map/psum | solution.py:8
  (128 shorter events, 63.1 us)
Async XLA Ops:
  7.2 301.9 %copy-start = (f32[4,4,128,128]{3,2,1,0:T(8,128)S(1)}, f32[4,4,128,128]{3,2,1,0:T(8,128)}, u32[]{:S(2)}) copy-start(f32[4,4,128,128]{3,2,1,0:T(8,128)} %param.11) | copy-start | bytes 3145732
  7.2 360.0 %reduce-scatter.3.cloned.1.call-start = ((), (), s32[]{:S(2)}) async-start(), calls=%async_computation.2 | async-start | bytes 655360 | tf_op jit(solution)/shard_map/reduce_scatter | solution.py:61
  7.2 12.9 collective-permute-start.2
  20.2 12.4 collective-permute-start.3
  37.0 18.7 %collective-permute-start = (f32[512,256]{1,0:T(8,128)S(1)}, f32[512,256]{1,0:T(8,128)S(1)}, u32[]{:S(2)}, u32[]{:S(2)}) collective-permute-start(f32[512,256]{1,0:T(8,128)S(1)} %get-tuple-element.223), channel_id=1, source_target_pairs={{0,4},{4,8},{8,12},{12,16},{16,20},{20,24},{24,28},{28,32},{32,36}... | collective-permute-start | bytes 1572872 | tf_op jit(solution)/shard_map/while/body/eval_jaxpr/ppermute | solution.py:16
  56.5 15.4 %collective-permute-start = (f32[512,256]{1,0:T(8,128)S(1)}, f32[512,256]{1,0:T(8,128)S(1)}, u32[]{:S(2)}, u32[]{:S(2)}) collective-permute-start(f32[512,256]{1,0:T(8,128)S(1)} %get-tuple-element.223), channel_id=1, source_target_pairs={{0,4},{4,8},{8,12},{12,16},{16,20},{20,24},{24,28},{28,32},{32,36}... | collective-permute-start | bytes 1572872 | tf_op jit(solution)/shard_map/while/body/eval_jaxpr/ppermute | solution.py:16
  72.8 14.4 collective-permute-start
  88.1 14.1 collective-permute-start
  103.1 14.1 collective-permute-start
  118.2 14.1 collective-permute-start
  133.2 14.1 collective-permute-start
  148.2 14.6 collective-permute-start
  163.7 15.7 %collective-permute-start = (f32[512,256]{1,0:T(8,128)S(1)}, f32[512,256]{1,0:T(8,128)S(1)}, u32[]{:S(2)}, u32[]{:S(2)}) collective-permute-start(f32[512,256]{1,0:T(8,128)S(1)} %get-tuple-element.223), channel_id=1, source_target_pairs={{0,4},{4,8},{8,12},{12,16},{16,20},{20,24},{24,28},{28,32},{32,36}... | collective-permute-start | bytes 1572872 | tf_op jit(solution)/shard_map/while/body/eval_jaxpr/ppermute | solution.py:16
  180.3 16.8 %collective-permute-start = (f32[512,256]{1,0:T(8,128)S(1)}, f32[512,256]{1,0:T(8,128)S(1)}, u32[]{:S(2)}, u32[]{:S(2)}) collective-permute-start(f32[512,256]{1,0:T(8,128)S(1)} %get-tuple-element.223), channel_id=1, source_target_pairs={{0,4},{4,8},{8,12},{12,16},{16,20},{20,24},{24,28},{28,32},{32,36}... | collective-permute-start | bytes 1572872 | tf_op jit(solution)/shard_map/while/body/eval_jaxpr/ppermute | solution.py:16
  198.0 17.9 %collective-permute-start = (f32[512,256]{1,0:T(8,128)S(1)}, f32[512,256]{1,0:T(8,128)S(1)}, u32[]{:S(2)}, u32[]{:S(2)}) collective-permute-start(f32[512,256]{1,0:T(8,128)S(1)} %get-tuple-element.223), channel_id=1, source_target_pairs={{0,4},{4,8},{8,12},{12,16},{16,20},{20,24},{24,28},{28,32},{32,36}... | collective-permute-start | bytes 1572872 | tf_op jit(solution)/shard_map/while/body/eval_jaxpr/ppermute | solution.py:16
  216.8 19.0 %collective-permute-start = (f32[512,256]{1,0:T(8,128)S(1)}, f32[512,256]{1,0:T(8,128)S(1)}, u32[]{:S(2)}, u32[]{:S(2)}) collective-permute-start(f32[512,256]{1,0:T(8,128)S(1)} %get-tuple-element.223), channel_id=1, source_target_pairs={{0,4},{4,8},{8,12},{12,16},{16,20},{20,24},{24,28},{28,32},{32,36}... | collective-permute-start | bytes 1572872 | tf_op jit(solution)/shard_map/while/body/eval_jaxpr/ppermute | solution.py:16
  236.6 19.7 %collective-permute-start = (f32[512,256]{1,0:T(8,128)S(1)}, f32[512,256]{1,0:T(8,128)S(1)}, u32[]{:S(2)}, u32[]{:S(2)}) collective-permute-start(f32[512,256]{1,0:T(8,128)S(1)} %get-tuple-element.223), channel_id=1, source_target_pairs={{0,4},{4,8},{8,12},{12,16},{16,20},{20,24},{24,28},{28,32},{32,36}... | collective-permute-start | bytes 1572872 | tf_op jit(solution)/shard_map/while/body/eval_jaxpr/ppermute | solution.py:16
  257.3 18.9 %collective-permute-start = (f32[512,256]{1,0:T(8,128)S(1)}, f32[512,256]{1,0:T(8,128)S(1)}, u32[]{:S(2)}, u32[]{:S(2)}) collective-permute-start(f32[512,256]{1,0:T(8,128)S(1)} %get-tuple-element.223), channel_id=1, source_target_pairs={{0,4},{4,8},{8,12},{12,16},{16,20},{20,24},{24,28},{28,32},{32,36}... | collective-permute-start | bytes 1572872 | tf_op jit(solution)/shard_map/while/body/eval_jaxpr/ppermute | solution.py:16
  277.0 17.9 %collective-permute-start = (f32[512,256]{1,0:T(8,128)S(1)}, f32[512,256]{1,0:T(8,128)S(1)}, u32[]{:S(2)}, u32[]{:S(2)}) collective-permute-start(f32[512,256]{1,0:T(8,128)S(1)} %get-tuple-element.223), channel_id=1, source_target_pairs={{0,4},{4,8},{8,12},{12,16},{16,20},{20,24},{24,28},{28,32},{32,36}... | collective-permute-start | bytes 1572872 | tf_op jit(solution)/shard_map/while/body/eval_jaxpr/ppermute | solution.py:16
  296.0 71.2 %copy-start.1 = (f32[128,256]{1,0:T(8,128)S(1)}, f32[128,256]{1,0:T(8,128)}, u32[]{:S(2)}) copy-start(f32[128,256]{1,0:T(8,128)} %param.15) | copy-start | bytes 393220
  296.0 71.2 %copy-start.3 = (f32[256,256]{1,0:T(8,128)S(1)}, f32[256,256]{1,0:T(8,128)}, u32[]{:S(2)}) copy-start(f32[256,256]{1,0:T(8,128)} %param.13) | copy-start | bytes 786436
  296.0 71.2 %copy-start.5 = (f32[256]{0:T(256)S(1)}, f32[256]{0:T(256)}, u32[]{:S(2)}) copy-start(f32[256]{0:T(256)} %param.14) | copy-start | bytes 3076
  311.5 982.6 %all-reduce.4.cloned.1.call-start = ((), (), s32[]{:S(2)}) async-start(), calls=%async_computation.4 | async-start | bytes 524288 | tf_op jit(solution)/shard_map/psum | solution.py:9
  393.0 3.2 copy-start.2
  396.2 251.0 %copy-start.4 = (f32[128,256]{1,0:T(8,128)S(1)}, f32[128,256]{1,0:T(8,128)}, u32[]{:S(2)}) copy-start(f32[128,256]{1,0:T(8,128)} %reduce-scatter.3.cloned.1.call-done) | copy-start | bytes 393220
  396.2 14.9 collective-permute-start.1
  411.3 18.6 %collective-permute-start.1 = (f32[512,256]{1,0:T(8,128)S(1)}, f32[512,256]{1,0:T(8,128)S(1)}, u32[]{:S(2)}, u32[]{:S(2)}) collective-permute-start(f32[512,256]{1,0:T(8,128)S(1)} %get-tuple-element.242), channel_id=1, source_target_pairs={{0,252},{4,0},{8,4},{12,8},{16,12},{20,16},{24,20},{28,24},{32,28}... | collective-permute-start | bytes 1572872 | tf_op jit(solution)/shard_map/while/body/eval_jaxpr/ppermute | solution.py:16
  429.9 17.6 %collective-permute-start.1 = (f32[512,256]{1,0:T(8,128)S(1)}, f32[512,256]{1,0:T(8,128)S(1)}, u32[]{:S(2)}, u32[]{:S(2)}) collective-permute-start(f32[512,256]{1,0:T(8,128)S(1)} %get-tuple-element.242), channel_id=1, source_target_pairs={{0,252},{4,0},{8,4},{12,8},{16,12},{20,16},{24,20},{28,24},{32,28}... | collective-permute-start | bytes 1572872 | tf_op jit(solution)/shard_map/while/body/eval_jaxpr/ppermute | solution.py:16
  447.6 16.7 %collective-permute-start.1 = (f32[512,256]{1,0:T(8,128)S(1)}, f32[512,256]{1,0:T(8,128)S(1)}, u32[]{:S(2)}, u32[]{:S(2)}) collective-permute-start(f32[512,256]{1,0:T(8,128)S(1)} %get-tuple-element.242), channel_id=1, source_target_pairs={{0,252},{4,0},{8,4},{12,8},{16,12},{20,16},{24,20},{28,24},{32,28}... | collective-permute-start | bytes 1572872 | tf_op jit(solution)/shard_map/while/body/eval_jaxpr/ppermute | solution.py:16
  464.4 15.8 %collective-permute-start.1 = (f32[512,256]{1,0:T(8,128)S(1)}, f32[512,256]{1,0:T(8,128)S(1)}, u32[]{:S(2)}, u32[]{:S(2)}) collective-permute-start(f32[512,256]{1,0:T(8,128)S(1)} %get-tuple-element.242), channel_id=1, source_target_pairs={{0,252},{4,0},{8,4},{12,8},{16,12},{20,16},{24,20},{28,24},{32,28}... | collective-permute-start | bytes 1572872 | tf_op jit(solution)/shard_map/while/body/eval_jaxpr/ppermute | solution.py:16
  480.3 14.9 collective-permute-start.1
  495.3 14.4 collective-permute-start.1
  509.8 14.1 collective-permute-start.1
  524.0 14.1 collective-permute-start.1
  538.2 14.1 collective-permute-start.1
  552.4 15.0 collective-permute-start.1
  567.5 16.1 %collective-permute-start.1 = (f32[512,256]{1,0:T(8,128)S(1)}, f32[512,256]{1,0:T(8,128)S(1)}, u32[]{:S(2)}, u32[]{:S(2)}) collective-permute-start(f32[512,256]{1,0:T(8,128)S(1)} %get-tuple-element.242), channel_id=1, source_target_pairs={{0,252},{4,0},{8,4},{12,8},{16,12},{20,16},{24,20},{28,24},{32,28}... | collective-permute-start | bytes 1572872 | tf_op jit(solution)/shard_map/while/body/eval_jaxpr/ppermute | solution.py:16
  583.7 17.2 %collective-permute-start.1 = (f32[512,256]{1,0:T(8,128)S(1)}, f32[512,256]{1,0:T(8,128)S(1)}, u32[]{:S(2)}, u32[]{:S(2)}) collective-permute-start(f32[512,256]{1,0:T(8,128)S(1)} %get-tuple-element.242), channel_id=1, source_target_pairs={{0,252},{4,0},{8,4},{12,8},{16,12},{20,16},{24,20},{28,24},{32,28}... | collective-permute-start | bytes 1572872 | tf_op jit(solution)/shard_map/while/body/eval_jaxpr/ppermute | solution.py:16
  600.9 18.2 %collective-permute-start.1 = (f32[512,256]{1,0:T(8,128)S(1)}, f32[512,256]{1,0:T(8,128)S(1)}, u32[]{:S(2)}, u32[]{:S(2)}) collective-permute-start(f32[512,256]{1,0:T(8,128)S(1)} %get-tuple-element.242), channel_id=1, source_target_pairs={{0,252},{4,0},{8,4},{12,8},{16,12},{20,16},{24,20},{28,24},{32,28}... | collective-permute-start | bytes 1572872 | tf_op jit(solution)/shard_map/while/body/eval_jaxpr/ppermute | solution.py:16
  619.2 19.3 %collective-permute-start.1 = (f32[512,256]{1,0:T(8,128)S(1)}, f32[512,256]{1,0:T(8,128)S(1)}, u32[]{:S(2)}, u32[]{:S(2)}) collective-permute-start(f32[512,256]{1,0:T(8,128)S(1)} %get-tuple-element.242), channel_id=1, source_target_pairs={{0,252},{4,0},{8,4},{12,8},{16,12},{20,16},{24,20},{28,24},{32,28}... | collective-permute-start | bytes 1572872 | tf_op jit(solution)/shard_map/while/body/eval_jaxpr/ppermute | solution.py:16
  638.6 8.4 collective-permute-start.4
  647.1 647.1 %collective-permute-start.5 = (f32[512,256]{1,0:T(8,128)S(1)}, f32[512,256]{1,0:T(8,128)S(1)}, u32[]{:S(2)}, u32[]{:S(2)}) collective-permute-start(f32[512,256]{1,0:T(8,128)S(1)} %broadcast_select_fusion), channel_id=1, source_target_pairs={{0,128},{4,132},{8,136},{12,140},{16,144},{20,148},{24,152},{28,15... | collective-permute-start | bytes 1572872 | tf_op jit(solution)/shard_map/ppermute | solution.py:16
  648.4 869.9 %all-reduce.6.cloned.1.call-start = ((), (), s32[]{:S(2)}) async-start(), calls=%async_computation.5 | async-start | bytes 524288 | tf_op jit(solution)/shard_map/psum | solution.py:8
  1294.2 224.1 %reduce-scatter.5.cloned.1.call-start = ((), (), s32[]{:S(2)}) async-start(), calls=%async_computation.3 | async-start | bytes 655360 | tf_op jit(solution)/shard_map/reduce_scatter | solution.py:95
Sparse Core Ops, SparseCore 0:
  311.6 55.4 reduce-scatter.2
  648.5 645.6 all-reduce.3
  1296.8 79.2 all-reduce.5
  1379.5 34.7 reduce-scatter.4
